TPU v7x, 32 devices: a whole 2x2x4 slice. The times are simulated.
32 devices in a mesh: lat: 2 (over y), lon: 16 (over z, x, core).
Axes of the slice: x: 2, y: 2, z: 4, core: 2. Of those that a mesh axis runs over, the one named last changes fastest.
Arguments:
- sea_level: float32 [2048, 256], P('lon', 'lat'), may hold values from -1 to 5
- east_velocity: float32 [2048, 256], P('lon', 'lat'), may hold values from -6 to 6
- north_velocity: float32 [2048, 256], P('lon', 'lat'), may hold values from -6 to 6
- depth: float32 [2048, 256], P('lon', 'lat'), may hold values from 0.25 to 1
- land_mask: int32 [2048, 256], P('lon', 'lat'), may hold values from 0 to 1, as said below
- wet_counts: int32 [2, 16], replicated, may hold values from 1 to 16384, as said below
- loading_prev: float32 [2048, 256], P('lon', 'lat'), may hold values from -4 to 4
- tide_amp: float32 [8], replicated, may hold values from 0.3 to 1
- tide_phase: float32 [8], replicated, may hold values from -3.140625 to 3.140625
- legendre: bfloat16 [512, 1024, 256], P('lon', None, 'lat'), may hold values from -0.375 to 0.375
- love_factor: float32 [1024], replicated, may hold values from 0.05 to 1
Outputs:
- height_new: float32 [2048, 256], P('lon', 'lat')
- east_new: float32 [2048, 256], P('lon', 'lat')
- north_new: float32 [2048, 256], P('lon', 'lat')
- self_attraction: float32 [2048, 256], P('lon', 'lat')
Inputs may be any that keep to these rules, and one draw needn't show every extreme that they name: `land_mask`: every tile of 128 columns by 128 rows holds at least one wet column, and one tile is wholly wet. wet_counts[p, q] is the number of wet columns of land_mask in latitude band p and longitude band q.
All inputs are finite; a program needn't handle non-finite values.
Results may differ from a plain program's by a relative error of at most 0.0038.
Values may be sent and summed in bfloat16 or wider, within the bound.
No kernel may reach another device: no remote copies, remote signals or barrier semaphores. Data moves between devices by JAX's collectives and lax.ppermute only.
A program may use at most 64 MiB of HBM per device.

v0:
```python
import math
import jax
import jax.numpy as jnp
from jax import lax
from jax.sharding import PartitionSpec as P

SUBSTEPS = 4
lat_edge = 1.3089969
courant = 0.4
friction = 0.02
rotation = 0.2
frequencies = (0.1405, 0.1454, 0.1379, 0.1458, 0.0729, 0.0676, 0.0725, 0.0649)
orders = (2, 2, 2, 2, 1, 1, 1, 1)
highest = lax.Precision.HIGHEST


def padded(cells, sides, width, closed):
    for axis, dim in sides:
        count = lax.axis_size(axis)
        ends = count if closed else count - 1
        head = lax.slice_in_dim(cells, 0, width, axis=dim)
        tail = lax.slice_in_dim(cells, cells.shape[dim] - width, cells.shape[dim], axis=dim)
        cells = jnp.concatenate(
            [
                lax.ppermute(tail, axis, [(i, (i + 1) % count) for i in range(ends)]),
                cells,
                lax.ppermute(head, axis, [((i + 1) % count, i) for i in range(ends)]),
            ],
            axis=dim,
        )
    return cells


def latitude_of(rows, total_rows):
    return -lat_edge + 2.0 * lat_edge * (rows.astype(jnp.float32) + 0.5) / total_rows


def potential(columns, rows, moment, total_cols, total_rows, tide_amp, tide_phase):
    longitude = (2.0 * math.pi * (columns % total_cols).astype(jnp.float32) / total_cols)[:, None]
    latitude = latitude_of(rows, total_rows)[None, :]
    semi = jnp.cos(latitude) ** 2
    diurnal = jnp.sin(2.0 * latitude)
    field = jnp.zeros((columns.shape[0], rows.shape[0]), jnp.float32)
    for index in range(len(frequencies)):
        shape_term = semi if orders[index] == 2 else diurnal
        field = field + tide_amp[index] * shape_term * jnp.cos(
            frequencies[index] * moment + orders[index] * longitude + tide_phase[index]
        )
    return field * (total_cols / 64.0)


def advance(state_x, static_x, forcing, latitude_x):
    height_x, east_x, north_x = (state_x[0], state_x[1], state_x[2])
    depth_x, wet_x, loading_x = (static_x[0], static_x[1], static_x[2])
    cosine = jnp.cos(latitude_x)[None, :]
    secant_cycle = (1.0 / jnp.cos(latitude_x[1:-1]))[None, :]
    secant_core = (1.0 / jnp.cos(latitude_x[2:-2]))[None, :]
    coriolis = (rotation * jnp.sin(latitude_x[2:-2]))[None, :]
    flux_east = depth_x * east_x
    flux_north = depth_x * north_x * cosine
    divergence = (
        (
            flux_east[2:, 1:-1]
            - flux_east[:-2, 1:-1]
            + (flux_north[1:-1, 2:] - flux_north[1:-1, :-2])
        )
        * 0.5
        * secant_cycle
    )
    height_cycle = height_x[1:-1, 1:-1] - courant * divergence * wet_x[1:-1, 1:-1]
    pressure = height_cycle - forcing - loading_x[1:-1, 1:-1]
    slope_east = (pressure[2:, 1:-1] - pressure[:-2, 1:-1]) * 0.5 * secant_core
    slope_north = (pressure[1:-1, 2:] - pressure[1:-1, :-2]) * 0.5
    east = east_x[2:-2, 2:-2]
    north = north_x[2:-2, 2:-2]
    wet = wet_x[2:-2, 2:-2]
    east_next = wet * ((1.0 - friction) * east + courant * (coriolis * north - slope_east))
    north_next = wet * ((1.0 - friction) * north - courant * (coriolis * east + slope_north))
    return jnp.stack([height_cycle[1:-1, 1:-1], east_next, north_next])


def extend_margin(fields, margin):
    wide = padded(fields, (("lon", 1),), margin, True)
    return padded(wide, (("lat", 2),), margin, False)


def wave_table(waves, columns, total_cols, weights):
    turns = waves[None, :] * columns[:, None] % total_cols
    angle = 2.0 * math.pi * turns.astype(jnp.float32) / total_cols
    scale = weights[None, :] / math.sqrt(total_cols)
    return jnp.stack([scale * jnp.cos(angle), -scale * jnp.sin(angle)], axis=2)


def shards(
    sea_level,
    east_velocity,
    north_velocity,
    depth,
    land_mask,
    wet_counts,
    loading_prev,
    tide_amp,
    tide_phase,
    legendre,
    love_factor,
):
    lon_dev, lat_dev = sea_level.shape
    wave_dev = legendre.shape[0]
    lon_count = lax.axis_size("lon")
    total_cols = lon_dev * lon_count
    total_rows = lat_dev * lax.axis_size("lat")
    lon_index = lax.axis_index("lon")
    lon_start = lon_index * lon_dev
    lat_start = lax.axis_index("lat") * lat_dev
    wet = land_mask.astype(jnp.float32)
    margin = 2 * SUBSTEPS
    full = extend_margin(
        jnp.stack([sea_level, east_velocity, north_velocity, depth, wet, loading_prev]), margin
    )
    state_x = full[:3]
    static_full = full[3:]
    wide_cols = full.shape[1]
    wide_rows = full.shape[2]
    for moment in range(SUBSTEPS):
        reach = margin - 2 * moment
        offset = margin - reach
        static_x = static_full[:, offset : wide_cols - offset, offset : wide_rows - offset]
        latitude_x = jnp.clip(
            latitude_of(
                lat_start + jnp.arange(-reach, lat_dev + reach, dtype=jnp.int32), total_rows
            ),
            -1.5,
            1.5,
        )
        columns = lon_start + jnp.arange(1 - reach, lon_dev + reach - 1, dtype=jnp.int32)
        rows = lat_start + jnp.arange(1 - reach, lat_dev + reach - 1, dtype=jnp.int32)
        forcing = potential(
            columns, rows, float(moment), total_cols, total_rows, tide_amp, tide_phase
        )
        state_x = advance(state_x, static_x, forcing, latitude_x)
    height = state_x[0]
    wet_sum = lax.psum(jnp.sum(wet * height), ("lat", "lon"))
    mean_level = wet_sum / jnp.sum(wet_counts.astype(jnp.float32))
    anomaly = wet * (height - mean_level)
    local_cols = lon_start + jnp.arange(lon_dev, dtype=jnp.int32)
    count = wave_dev * lax.axis_size("lon")
    waves = jnp.arange(count, dtype=jnp.int32)
    table = wave_table(waves, local_cols, total_cols, jnp.ones((count,), jnp.float32))
    table = jnp.transpose(table, (1, 2, 0)).reshape(2 * count, lon_dev)
    fourier = lax.psum_scatter(
        jnp.dot(table, anomaly, precision=highest, preferred_element_type=jnp.float32).reshape(
            count, 2, lat_dev
        ),
        "lon",
        scatter_dimension=0,
        tiled=True,
    ).astype(jnp.bfloat16)
    coefficients = lax.dot_general(
        fourier, legendre, (((2,), (2,)), ((0,), (0,))), preferred_element_type=jnp.float32
    )
    coefficients = lax.psum(coefficients, "lat")
    scaled = (coefficients * love_factor[None, None, :]).astype(jnp.bfloat16)
    synthesis = lax.dot_general(
        scaled, legendre, (((2,), (1,)), ((0,), (0,))), preferred_element_type=jnp.float32
    )
    own_waves = lon_index * wave_dev + jnp.arange(wave_dev, dtype=jnp.int32)
    weights = jnp.where(own_waves == 0, 1.0, 2.0).astype(jnp.float32)
    flat_spectra = synthesis.reshape(2 * wave_dev, lat_dev)
    count = lon_dev * lax.axis_size("lon")
    cells = jnp.arange(count, dtype=jnp.int32)
    table = wave_table(own_waves, cells, total_cols, weights).reshape(count, 2 * wave_dev)
    self_attraction = lax.psum_scatter(
        jnp.dot(table, flat_spectra, precision=highest, preferred_element_type=jnp.float32),
        "lon",
        scatter_dimension=0,
        tiled=True,
    )
    return (state_x[0], state_x[1], state_x[2], self_attraction)


def solution(mesh):
    placed = (
        P("lon", "lat"),
        P("lon", "lat"),
        P("lon", "lat"),
        P("lon", "lat"),
        P("lon", "lat"),
        P(),
        P("lon", "lat"),
        P(),
        P(),
        P("lon", None, "lat"),
        P(),
    )
    return jax.shard_map(
        shards,
        mesh=mesh,
        in_specs=placed,
        out_specs=(P("lon", "lat"), P("lon", "lat"), P("lon", "lat"), P("lon", "lat")),
        check_vma=False,
    )
```

profile of v0, /device:TPU:0, one launch (start us, length us, event | category | flops | bytes accessed | tf_op | source)
XLA Modules:
  0.0 292.7 jit_solution(6166529491891947540)
XLA Ops:
  12.8 5.0 %collective-permute-start.1 = (f32[6,8,128]{2,1,0:T(8,128)S(1)}, f32[6,8,128]{2,1,0:T(8,128)S(1)}, u32[]{:S(2)}, u32[]{:S(2)}) collective-permute-start(f32[6,8,128]{2,1,0:T(8,128)S(1)} %get-tuple-element.50), channel_id=1, source_target_pairs={{1,0},{2,1},{3,2},{4,3},{5,4},{6,5},{7,6},{8,7},{9,8},{10,9},{11,1... | collective-permute-start | bytes 73736 | tf_op jit(solution)/shard_map/ppermute | solution.py:27
  18.2 1.6 fusion.116
  30.0 1.6 fusion.117
  31.6 1.4 add_cosine_fusion.28
  33.0 1.4 add_cosine_fusion.20
  37.0 1.4 add_cosine_fusion.24
  38.4 1.4 add_cosine_fusion.16
  41.1 1.4 add_cosine_fusion.18
  47.9 1.4 add_cosine_fusion.8
  49.2 1.4 add_cosine_fusion.10
  50.6 1.4 add_cosine_fusion.12
  58.7 1.4 add_cosine_fusion
  60.1 1.4 add_cosine_fusion.2
  61.4 1.4 add_cosine_fusion.4
  66.9 4.0 %collective-permute-start.2 = (f32[6,144,8]{2,1,0:T(8,128)S(1)}, f32[6,144,8]{2,1,0:T(8,128)S(1)}, u32[]{:S(2)}, u32[]{:S(2)}) collective-permute-start(f32[6,144,8]{2,1,0:T(8,128)S(1)} %get-tuple-element.47), channel_id=1, source_target_pairs={{0,16},{1,17},{2,18},{3,19},{4,20},{5,21},{6,22},{7,23},{8,24},{9,... | collective-permute-start | bytes 82952 | tf_op jit(solution)/shard_map/ppermute | solution.py:25
  74.2 3.5 %collective-permute-done.2 = f32[6,144,8]{2,1,0:T(8,128)S(1)} collective-permute-done((f32[6,144,8]{2,1,0:T(8,128)S(1)}, f32[6,144,8]{2,1,0:T(8,128)S(1)}, u32[]{:S(2)}, u32[]{:S(2)}) %collective-permute-start.2) | collective-permute-done | bytes 27680 | tf_op jit(solution)/shard_map/ppermute | solution.py:25
  77.7 4.1 %collective-permute-done.3 = f32[6,144,8]{2,1,0:T(8,128)S(1)} collective-permute-done((f32[6,144,8]{2,1,0:T(8,128)S(1)}, f32[6,144,8]{2,1,0:T(8,128)S(1)}, u32[]{:S(2)}, u32[]{:S(2)}) %collective-permute-start.3) | collective-permute-done | bytes 27680 | tf_op jit(solution)/shard_map/ppermute | solution.py:27
  86.3 39.7 %psum.14 = f32[]{:T(128)} all-reduce(f32[]{:T(128)} %get-tuple-element.4), channel_id=1, replica_groups=mesh['lat'=2,'lon'=16] {'lat','lon'}, use_global_device_ids=true, to_apply=%region_1.2 | all-reduce | flops 1 | bytes 8 | tf_op jit(solution)/shard_map/psum | solution.py:142
  128.8 65.7 %all-reduce.5 = bf16[512,2,128]{2,1,0:T(2,128)(2,1)S(1)} all-reduce(f32[512,2,128]{2,1,0:T(2,128)S(1)} %copy.15), channel_id=2, replica_groups=mesh['lat'=2,'lon'=16] {'lon'}, use_global_device_ids=true, to_apply=%region_3.4.clone | all-reduce | flops 131072 | bytes 786432
  194.5 6.4 %fusion.86 = f32[32,2,1024]{2,1,0:T(2,128)} fusion(bf16[32,1024,128]{2,1,0:T(8,128)(2,1)} %param.20, bf16[512,2,128]{2,1,0:T(2,128)(2,1)S(1)} %all-reduce.5, u32[]{:T(128)S(6)} %multiply.402), kind=kOutput, calls=%fused_computation.152 | convolution fusion | flops 16777216 | bytes 8667140 | tf_op jit(solution)/shard_map/dot_general | solution.py:158
  202.2 18.4 %all-reduce.4.cloned.1.call-done = f32[32,2,1024]{2,1,0:T(2,128)} async-done(((f32[32,2,1024]{2,1,0:T(2,128)}), f32[32,2,1024]{2,1,0:T(2,128)}) %all-reduce.4.cloned.1.call-update) | async-done | bytes 262160 | tf_op jit(solution)/shard_map/psum | solution.py:161
  220.6 4.7 %fusion.66 = f32[32,2,128]{2,1,0:T(2,128)S(1)} fusion(bf16[32,1024,128]{2,1,0:T(8,128)(2,1)} %param.20, f32[32,2,1024]{2,1,0:T(2,128)} %all-reduce.4.cloned.1.call-done, f32[1024]{0:T(1024)S(1)} %copy-done.2), kind=kOutput, calls=%fused_computation.122 | convolution fusion | flops 16908288 | bytes 8687616 | tf_op jit(solution)/shard_map/dot_general | solution.py:163
  225.3 2.8 convolution_bitcast_fusion
  229.1 56.8 %reduce-scatter.2.cloned.1.call-done = f32[128,128]{1,0:T(8,128)} async-done(((f32[2048,128]{1,0:T(8,128)}), f32[128,128]{1,0:T(8,128)}) %reduce-scatter.2.cloned.1.call-update) | async-done | bytes 65552 | tf_op jit(solution)/shard_map/reduce_scatter | solution.py:172
  (80 shorter events, 46.9 us)
Async XLA Ops:
  7.2 213.4 %all-reduce.4.cloned.1.call-start = ((), (), s32[]{:S(2)}) async-start(), calls=%async_computation.1 | async-start | bytes 524288 | tf_op jit(solution)/shard_map/psum | solution.py:161
  12.3 54.4 %collective-permute-start = (f32[6,8,128]{2,1,0:T(8,128)S(1)}, f32[6,8,128]{2,1,0:T(8,128)S(1)}, u32[]{:S(2)}, u32[]{:S(2)}) collective-permute-start(f32[6,8,128]{2,1,0:T(8,128)S(1)} %get-tuple-element.49), channel_id=1, source_target_pairs={{0,1},{1,2},{2,3},{3,4},{4,5},{5,6},{6,7},{7,8},{8,9},{9,10},{10,1... | collective-permute-start | bytes 73736 | tf_op jit(solution)/shard_map/ppermute | solution.py:25
  12.8 53.9 %collective-permute-start.1 = (f32[6,8,128]{2,1,0:T(8,128)S(1)}, f32[6,8,128]{2,1,0:T(8,128)S(1)}, u32[]{:S(2)}, u32[]{:S(2)}) collective-permute-start(f32[6,8,128]{2,1,0:T(8,128)S(1)} %get-tuple-element.50), channel_id=1, source_target_pairs={{1,0},{2,1},{3,2},{4,3},{5,4},{6,5},{7,6},{8,7},{9,8},{10,9},{11,1... | collective-permute-start | bytes 73736 | tf_op jit(solution)/shard_map/ppermute | solution.py:27
  66.9 18.7 %copy-start = (s32[128,128]{1,0:T(8,128)S(1)}, s32[128,128]{1,0:T(8,128)}, u32[]{:S(2)}) copy-start(s32[128,128]{1,0:T(8,128)} %param.15) | copy-start | bytes 196612
  66.9 10.7 %collective-permute-start.2 = (f32[6,144,8]{2,1,0:T(8,128)S(1)}, f32[6,144,8]{2,1,0:T(8,128)S(1)}, u32[]{:S(2)}, u32[]{:S(2)}) collective-permute-start(f32[6,144,8]{2,1,0:T(8,128)S(1)} %get-tuple-element.47), channel_id=1, source_target_pairs={{0,16},{1,17},{2,18},{3,19},{4,20},{5,21},{6,22},{7,23},{8,24},{9,... | collective-permute-start | bytes 82952 | tf_op jit(solution)/shard_map/ppermute | solution.py:25
  70.9 10.9 %collective-permute-start.3 = (f32[6,144,8]{2,1,0:T(8,128)S(1)}, f32[6,144,8]{2,1,0:T(8,128)S(1)}, u32[]{:S(2)}, u32[]{:S(2)}) collective-permute-start(f32[6,144,8]{2,1,0:T(8,128)S(1)} %get-tuple-element.48), channel_id=1, source_target_pairs={{16,0},{17,1},{18,2},{19,3},{20,4},{21,5},{22,6},{23,7},{24,8},{25... | collective-permute-start | bytes 82952 | tf_op jit(solution)/shard_map/ppermute | solution.py:27
  84.4 136.2 %copy-start.2 = (f32[1024]{0:T(1024)S(1)}, f32[1024]{0:T(1024)}, u32[]{:S(2)}) copy-start(f32[1024]{0:T(1024)} %param.21) | copy-start | bytes 12292
  86.3 138.9 %copy-start.1 = (f32[128,128]{1,0:T(8,128)}, f32[128,128]{1,0:T(8,128)S(1)}, u32[]{:S(2)}) copy-start(f32[128,128]{1,0:T(8,128)S(1)} %get-tuple-element.5) | copy-start | bytes 196612
  200.9 85.0 %reduce-scatter.2.cloned.1.call-start = ((), (), s32[]{:S(2)}) async-start(), calls=%async_computation.2 | async-start | bytes 1114112 | tf_op jit(solution)/shard_map/reduce_scatter | solution.py:172
Sparse Core Ops, SparseCore 0:
  201.0 19.5 all-reduce.3
  228.2 57.5 reduce-scatter.1
where the time goes:
time: 294 us; the launch traced here: 293 us
  blocking collectives  105 us (36%)
  waiting for transfers between devices  82.9 us (28%)
  other arithmetic  52.3 us (18%)
  between operations  16.4 us (6%)
  matrix products  14.9 us (5%)
  starting transfers between devices  11.1 us (4%)
  local copies, waits for them, and re-layouts  9.8 us (3%)
    unnamed x1, blocking collectives  65.7 us
    reduce_scatter x1, waiting for transfers between devices, shards(): lax.psum_scatter(jnp.dot(table, flat_spectra, precision=highest, preferre...  56.8 us
    psum x1, blocking collectives, shards(): wet_sum = lax.psum(jnp.sum(wet * height), ('lat', 'lon'))  39.7 us
    cos x16, other arithmetic, potential(): jnp.cos(frequencies[index] * moment + orders[index] * longitude + tide_ph...  21.7 us
    mul x16, other arithmetic, potential(): tide_amp[index] * shape_term  20.3 us
    psum x1, waiting for transfers between devices, shards(): coefficients = lax.psum(coefficients, 'lat')  18.4 us
    dot_general x1, matrix products, shards(): lax.dot_general(fourier, legendre, (((2,), (2,)), ((0,), (0,))), preferre...  6.37 us
    ppermute x2, starting transfers between devices, padded(): lax.ppermute(head, axis, [((i + 1) % count, i) for i in range(ends)])  6.31 us
  transfers between devices with their start and end apart: 6, of which 4 were waited for; matrix products, arithmetic and copies ran while one was open for 18% of the time, Pallas kernels for 0%

commit v1 on v0

--- a/solution.py
+++ b/solution.py
@@ -158,7 +158,7 @@
     coefficients = lax.dot_general(
         fourier, legendre, (((2,), (2,)), ((0,), (0,))), preferred_element_type=jnp.float32
     )
-    coefficients = lax.psum(coefficients, "lat")
+    coefficients = jnp.sum(lax.all_gather(coefficients, "lat"), axis=0)
     scaled = (coefficients * love_factor[None, None, :]).astype(jnp.bfloat16)
     synthesis = lax.dot_general(
         scaled, legendre, (((2,), (1,)), ((0,), (0,))), preferred_element_type=jnp.float32

time: 294 us -> 280 us (0.952)
  waiting for transfers between devices: 82.9 us -> 61.2 us
  blocking collectives: 105 us -> 113 us
    psum x1 -> x0, waiting for transfers between devices: 18.4 us -> none  [shards(): coefficients = lax.psum(coefficients, 'lat')]
    all_gather x0 -> x1, blocking collectives: none -> 7.03 us  [shards(): coefficients = jnp.sum(lax.all_gather(coefficients, 'lat'), axis=0)]
  transfers between devices with their start and end apart: 6 -> 5, of which waited for: 4 -> 3; matrix products, arithmetic and copies ran while one was open for 18% -> 19% of each run, Pallas kernels for 0% -> 0%
where the time goes in v1:
time: 280 us; the launch traced here: 279 us
  blocking collectives  113 us (40%)
  waiting for transfers between devices  61.2 us (22%)
  other arithmetic  54 us (19%)
  between operations  16.4 us (6%)
  matrix products  14.1 us (5%)
  starting transfers between devices  10.9 us (4%)
  local copies, waits for them, and re-layouts  9.8 us (4%)
    unnamed x1, blocking collectives  65.9 us
    reduce_scatter x1, waiting for transfers between devices, shards(): lax.psum_scatter(jnp.dot(table, flat_spectra, precision=highest, preferre...  54.8 us
    psum x1, blocking collectives, shards(): wet_sum = lax.psum(jnp.sum(wet * height), ('lat', 'lon'))  39.7 us
    cos x16, other arithmetic, potential(): jnp.cos(frequencies[index] * moment + orders[index] * longitude + tide_ph...  21.2 us
    mul x16, other arithmetic, potential(): tide_amp[index] * shape_term  21.2 us
    all_gather x1, blocking collectives, shards(): coefficients = jnp.sum(lax.all_gather(coefficients, 'lat'), axis=0)  7.03 us
    ppermute x2, starting transfers between devices, padded(): lax.ppermute(head, axis, [((i + 1) % count, i) for i in range(ends)])  6.31 us
    dot_general x1, matrix products, shards(): lax.dot_general(fourier, legendre, (((2,), (2,)), ((0,), (0,))), preferre...  5.66 us
  transfers between devices with their start and end apart: 5, of which 3 were waited for; matrix products, arithmetic and copies ran while one was open for 19% of the time, Pallas kernels for 0%

profile of v1, /device:TPU:0, one launch (start us, length us, event | category | flops | bytes accessed | tf_op | source)
XLA Modules:
  0.0 279.0 jit_solution(10400572264948385921)
XLA Ops:
  12.8 5.0 %collective-permute-start.1 = (f32[6,8,128]{2,1,0:T(8,128)S(1)}, f32[6,8,128]{2,1,0:T(8,128)S(1)}, u32[]{:S(2)}, u32[]{:S(2)}) collective-permute-start(f32[6,8,128]{2,1,0:T(8,128)S(1)} %get-tuple-element.50), channel_id=1, source_target_pairs={{1,0},{2,1},{3,2},{4,3},{5,4},{6,5},{7,6},{8,7},{9,8},{10,9},{11,1... | collective-permute-start | bytes 73736 | tf_op jit(solution)/shard_map/ppermute | solution.py:27
  18.2 1.6 fusion.116
  19.8 1.4 broadcast_multiply_fusion.30
  21.3 1.4 broadcast_multiply_fusion.20
  30.4 1.6 fusion.117
  39.9 1.4 add_cosine_fusion.26
  41.3 1.4 add_cosine_fusion.18
  42.9 1.4 broadcast_multiply_fusion.10
  48.2 1.3 add_cosine_fusion.8
  49.6 1.4 add_cosine_fusion.10
  53.8 1.4 broadcast_multiply_fusion
  59.1 1.3 add_cosine_fusion
  60.4 1.4 add_cosine_fusion.2
  67.0 4.0 %collective-permute-start.2 = (f32[6,144,8]{2,1,0:T(8,128)S(1)}, f32[6,144,8]{2,1,0:T(8,128)S(1)}, u32[]{:S(2)}, u32[]{:S(2)}) collective-permute-start(f32[6,144,8]{2,1,0:T(8,128)S(1)} %get-tuple-element.47), channel_id=1, source_target_pairs={{0,16},{1,17},{2,18},{3,19},{4,20},{5,21},{6,22},{7,23},{8,24},{9,... | collective-permute-start | bytes 82952 | tf_op jit(solution)/shard_map/ppermute | solution.py:25
  75.5 2.2 collective-permute-done.2
  77.7 4.2 %collective-permute-done.3 = f32[6,144,8]{2,1,0:T(8,128)} collective-permute-done((f32[6,144,8]{2,1,0:T(8,128)S(1)}, f32[6,144,8]{2,1,0:T(8,128)}, u32[]{:S(2)}, u32[]{:S(2)}) %collective-permute-start.3) | collective-permute-done | bytes 27680 | tf_op jit(solution)/shard_map/ppermute | solution.py:27
  82.0 1.4 pad_maximum_fusion
  87.5 39.7 %psum.7 = f32[]{:T(128)} all-reduce(f32[]{:T(128)} %get-tuple-element.4), channel_id=1, replica_groups=mesh['lat'=2,'lon'=16] {'lat','lon'}, use_global_device_ids=true, to_apply=%region_1.2 | all-reduce | flops 1 | bytes 8 | tf_op jit(solution)/shard_map/psum | solution.py:142
  130.0 65.9 %all-reduce.2 = bf16[512,2,128]{2,1,0:T(2,128)(2,1)S(1)} all-reduce(f32[512,2,128]{2,1,0:T(2,128)S(1)} %copy.15), channel_id=3, replica_groups=mesh['lat'=2,'lon'=16] {'lon'}, use_global_device_ids=true, to_apply=%region_3.4.clone | all-reduce | flops 131072 | bytes 786432
  195.8 5.7 %fusion.86 = f32[32,2,1024]{2,1,0:T(2,128)S(1)} fusion(bf16[32,1024,128]{2,1,0:T(8,128)(2,1)} %param.20, bf16[512,2,128]{2,1,0:T(2,128)(2,1)S(1)} %all-reduce.2, u32[]{:T(128)S(6)} %multiply.402), kind=kOutput, calls=%fused_computation.152 | convolution fusion | flops 16777216 | bytes 8667140 | tf_op jit(solution)/shard_map/dot_general | solution.py:158
  201.5 7.0 %all-gather = f32[64,2,1024]{2,1,0:T(2,128)S(1)} all-gather(f32[32,2,1024]{2,1,0:T(2,128)S(1)} %fusion.86), channel_id=2, replica_groups=mesh['lat'=2,'lon'=16] {'lat'}, dimensions={0}, use_global_device_ids=true | all-gather | bytes 786432 | tf_op jit(solution)/shard_map/all_gather | solution.py:161
  209.0 4.6 %fusion.66 = f32[32,2,128]{2,1,0:T(2,128)S(1)} fusion(bf16[32,1024,128]{2,1,0:T(8,128)(2,1)} %param.20, f32[32,2,1024]{2,1,0:T(2,128)S(1)} %reduce_sum.29, f32[1024]{0:T(1024)S(1)} %copy-done.2), kind=kOutput, calls=%fused_computation.122 | convolution fusion | flops 16908288 | bytes 8687616 | tf_op jit(solution)/shard_map/dot_general | solution.py:163
  213.6 2.8 %convolution_bitcast_fusion = f32[2048,128]{1,0:T(8,128)} fusion(f32[2048,32,1]{0,1,2:T(8,128)S(1)} %get-tuple-element.62, f32[2048,32,1]{0,1,2:T(8,128)S(1)} %get-tuple-element.61, f32[32,2,128]{2,1,0:T(2,128)S(1)} %fusion.66), kind=kOutput, calls=%fused_computation | convolution fusion | flops 201457664 | bytes 1605632 | tf_op jit(solution)/shard_map/dot_general | solution.py:173
  217.4 54.8 %reduce-scatter.2.cloned.1.call-done = f32[128,128]{1,0:T(8,128)} async-done(((f32[2048,128]{1,0:T(8,128)}), f32[128,128]{1,0:T(8,128)}) %reduce-scatter.2.cloned.1.call-update) | async-done | bytes 65552 | tf_op jit(solution)/shard_map/reduce_scatter | solution.py:172
  (79 shorter events, 48.2 us)
Async XLA Ops:
  7.2 264.9 %reduce-scatter.2.cloned.1.call-start = ((), (), s32[]{:S(2)}) async-start(), calls=%async_computation.1 | async-start | bytes 1114112 | tf_op jit(solution)/shard_map/reduce_scatter | solution.py:172
  12.3 54.5 %collective-permute-start = (f32[6,8,128]{2,1,0:T(8,128)S(1)}, f32[6,8,128]{2,1,0:T(8,128)S(1)}, u32[]{:S(2)}, u32[]{:S(2)}) collective-permute-start(f32[6,8,128]{2,1,0:T(8,128)S(1)} %get-tuple-element.49), channel_id=1, source_target_pairs={{0,1},{1,2},{2,3},{3,4},{4,5},{5,6},{6,7},{7,8},{8,9},{9,10},{10,1... | collective-permute-start | bytes 73736 | tf_op jit(solution)/shard_map/ppermute | solution.py:25
  12.8 53.9 %collective-permute-start.1 = (f32[6,8,128]{2,1,0:T(8,128)S(1)}, f32[6,8,128]{2,1,0:T(8,128)S(1)}, u32[]{:S(2)}, u32[]{:S(2)}) collective-permute-start(f32[6,8,128]{2,1,0:T(8,128)S(1)} %get-tuple-element.50), channel_id=1, source_target_pairs={{1,0},{2,1},{3,2},{4,3},{5,4},{6,5},{7,6},{8,7},{9,8},{10,9},{11,1... | collective-permute-start | bytes 73736 | tf_op jit(solution)/shard_map/ppermute | solution.py:27
  67.0 19.8 %copy-start = (s32[128,128]{1,0:T(8,128)S(1)}, s32[128,128]{1,0:T(8,128)}, u32[]{:S(2)}) copy-start(s32[128,128]{1,0:T(8,128)} %param.15) | copy-start | bytes 196612
  67.0 10.7 %collective-permute-start.2 = (f32[6,144,8]{2,1,0:T(8,128)S(1)}, f32[6,144,8]{2,1,0:T(8,128)S(1)}, u32[]{:S(2)}, u32[]{:S(2)}) collective-permute-start(f32[6,144,8]{2,1,0:T(8,128)S(1)} %get-tuple-element.47), channel_id=1, source_target_pairs={{0,16},{1,17},{2,18},{3,19},{4,20},{5,21},{6,22},{7,23},{8,24},{9,... | collective-permute-start | bytes 82952 | tf_op jit(solution)/shard_map/ppermute | solution.py:25
  71.0 11.0 %collective-permute-start.3 = (f32[6,144,8]{2,1,0:T(8,128)S(1)}, f32[6,144,8]{2,1,0:T(8,128)}, u32[]{:S(2)}, u32[]{:S(2)}) collective-permute-start(f32[6,144,8]{2,1,0:T(8,128)S(1)} %get-tuple-element.48), channel_id=1, source_target_pairs={{16,0},{17,1},{18,2},{19,3},{20,4},{21,5},{22,6},{23,7},{24,8},{25... | collective-permute-start | bytes 82952 | tf_op jit(solution)/shard_map/ppermute | solution.py:27
  86.0 123.0 %copy-start.2 = (f32[1024]{0:T(1024)S(1)}, f32[1024]{0:T(1024)}, u32[]{:S(2)}) copy-start(f32[1024]{0:T(1024)} %param.21) | copy-start | bytes 12292
  87.5 126.1 %copy-start.1 = (f32[128,128]{1,0:T(8,128)}, f32[128,128]{1,0:T(8,128)S(1)}, u32[]{:S(2)}) copy-start(f32[128,128]{1,0:T(8,128)S(1)} %get-tuple-element.5) | copy-start | bytes 196612
Sparse Core Ops, SparseCore 0:
  216.5 55.5 reduce-scatter.1
